TPU v7x, 512 devices: a whole 4x4x16 slice. The times are simulated.
512 devices in a mesh: frame: 16 (over z), dom: 8 (over x, core), coef: 4 (over y).
Axes of the slice: x: 4, y: 4, z: 16, core: 2. Of those that a mesh axis runs over, the one named last changes fastest.
Arguments:
- geometry: float32 [32, 524288], P('coef', ('frame', 'dom')), may hold values from -1 to 1
- fraction: float32 [32, 524288], P('coef', ('frame', 'dom')), may hold values from 0 to 1
- interval: int32 [32, 524288], P('coef', ('frame', 'dom')), may hold values from 0 to 156
- pattern: int32 [32, 4096], P('coef', ('frame', 'dom')), may hold values from 0 to 95
- target: float32 [524288], P(('frame', 'dom')), may hold values from -8 to 8
Outputs:
- solution: float32 [384, 160], P('coef')
- residual: float32 [524288], P(('frame', 'dom'))
Inputs may be any that keep to these rules, and one draw needn't show every extreme that they name: The spline of a slot reads coefficients interval to interval + 3 of its type. Slot s refers to pair type (s // 8) * 96 + pattern.
All inputs are finite; a program needn't handle non-finite values.
Results may differ from a plain program's by a relative error of at most 0.0003.
Values sent between devices are 32-bit elements; how exact they have to be, the bound alone decides.
No kernel may reach another device: no remote copies, remote signals or barrier semaphores. Data moves between devices by JAX's collectives and lax.ppermute only.
A program may use at most 64 MiB of HBM per device.

v0:
```python
import math
import jax
import jax.numpy as jnp
from jax import lax
from jax.sharding import PartitionSpec as P

NK = 160
TYPES = 384
ITERS = 2


def spline_weights(fraction):
    square = fraction * fraction
    cube = square * fraction
    return (
        (1.0 - fraction) ** 3 / 6.0,
        (3.0 * cube - 6.0 * square + 4.0) / 6.0,
        (-3.0 * cube + 3.0 * square + 3.0 * fraction + 1.0) / 6.0,
        cube / 6.0,
    )


def dense_tiles(geom, fraction, interval):
    knots = lax.broadcasted_iota(jnp.int32, (1, NK, 1), 1)
    tiles = jnp.zeros((geom.shape[0], NK, geom.shape[1]), jnp.float32)
    for offset, weight in enumerate(spline_weights(fraction)):
        hit = knots == (interval + offset)[:, None, :]
        tiles = tiles + jnp.where(hit, (geom * weight)[:, None, :], 0.0)
    return tiles


def block_layout(geom):
    tiles_all = geom.shape[1] // 128
    block = math.gcd(8, tiles_all)
    return (block, block * 128, tiles_all // block)


def block_tiles(geometry, fraction, interval, pattern, index, block, width):
    start = index * width
    geom = lax.dynamic_slice_in_dim(geometry, start, width, 1)
    frac = lax.dynamic_slice_in_dim(fraction, start, width, 1)
    knot = lax.dynamic_slice_in_dim(interval, start, width, 1)
    kinds = lax.dynamic_slice_in_dim(pattern, index * block, block, 1)
    tiles = dense_tiles(geom, frac, knot).reshape(geom.shape[0], NK, block, 128)
    return (tiles, kinds, start)


def forward(coeffs, geometry, fraction, interval, pattern):
    block, width, count = block_layout(geometry)

    def forward_step(index, image):
        tiles, kinds, start = block_tiles(
            geometry, fraction, interval, pattern, index, block, width
        )
        chosen = jnp.take(coeffs, kinds, axis=0)
        part = jnp.einsum("sktr,stk->tr", tiles, chosen, precision=lax.Precision.HIGHEST)
        return lax.dynamic_update_slice_in_dim(image, part.reshape(width), start, 0)

    return lax.fori_loop(0, count, forward_step, jnp.zeros((geometry.shape[1],), jnp.float32))


def backward(resid, per_coef, geometry, fraction, interval, pattern):
    block, width, count = block_layout(geometry)
    owners = lax.broadcasted_iota(jnp.int32, (1, 1, per_coef), 2)

    def backward_step(index, total):
        tiles, kinds, start = block_tiles(
            geometry, fraction, interval, pattern, index, block, width
        )
        piece = lax.dynamic_slice_in_dim(resid, start, width, 0).reshape(block, 128)
        contrib = jnp.einsum("sktr,tr->stk", tiles, piece, precision=lax.Precision.HIGHEST)
        picks = (kinds[:, :, None] == owners).astype(jnp.float32)
        return total + jnp.einsum("stc,stk->ck", picks, contrib, precision=lax.Precision.HIGHEST)

    return lax.fori_loop(0, count, backward_step, jnp.zeros((per_coef, NK), jnp.float32))


def on_device(geometry, fraction, interval, pattern, target):
    per_coef = TYPES // lax.axis_size("coef")

    def transpose_sum(resid):
        local = backward(resid, per_coef, geometry, fraction, interval, pattern).reshape(
            per_coef * NK
        )
        share = lax.psum(local, ("frame", "dom"))
        total = lax.psum(jnp.sum(share * share), "coef")
        return (share, total)

    def expand(share):
        return share.reshape(per_coef, NK)

    residual = target
    gradient, gamma = transpose_sum(residual)
    direction = gradient
    solution = jnp.zeros_like(gradient)
    for step_index in range(ITERS):
        partial_image = forward(expand(direction), geometry, fraction, interval, pattern)
        image = lax.psum(partial_image, "coef")
        image_total = lax.psum(jnp.sum(image * image), ("frame", "dom"))
        alpha = gamma / image_total
        solution = solution + alpha * direction
        residual = residual - alpha * image
        if step_index + 1 < ITERS:
            gradient, gamma_next = transpose_sum(residual)
            direction = gradient + gamma_next / gamma * direction
            gamma = gamma_next
    return (expand(solution), residual)


def solution(mesh):
    in_specs = (
        P("coef", ("frame", "dom")),
        P("coef", ("frame", "dom")),
        P("coef", ("frame", "dom")),
        P("coef", ("frame", "dom")),
        P(("frame", "dom")),
    )
    out_specs = (P("coef", None), P(("frame", "dom")))
    return jax.shard_map(
        on_device, mesh=mesh, in_specs=in_specs, out_specs=out_specs, check_vma=False
    )
```

profile of v0, /device:TPU:1, one launch (start us, length us, event | category | flops | bytes accessed | tf_op | source)
XLA Modules:
  0.0 1750.1 jit_solution(9884929640221820795)
XLA Ops:
  0.6 52.4 %while.56 = (s32[]{:T(128)}, f32[96,160]{0,1:T(8,128)S(1)}, s32[8,32]{1,0:T(8,128)}, f32[4096]{0:T(1024)}, s32[8,4096]{1,0:T(8,128)}, /*index=5*/f32[8,4096]{1,0...) while((s32[]{:T(128)}, f32[96,160]{0,1:T(8,128)S(1)}, ...), condition=%wide.region_1.2_spmd.clone, body=%wide.region_0.1_spmd.clone.sunk | while | flops 42192900 | bytes 11854863 | solution.py:75
  0.7 0.8 fusion.117
  2.4 1.9 select_add_fusion.10
  5.0 8.4 fusion.118
  13.8 0.8 fusion.117
  15.5 1.9 select_add_fusion.10
  18.1 8.4 fusion.118
  26.9 0.8 fusion.117
  28.6 1.9 select_add_fusion.10
  31.2 8.4 fusion.118
  41.7 1.9 select_add_fusion.10
  44.3 8.4 fusion.118
  53.3 498.0 %psum.56 = f32[15360]{0:T(1024)S(1)} all-reduce(f32[15360]{0:T(1024)S(1)} %reshape.226), channel_id=1, replica_groups=mesh['frame'=16,'dom'=8,'coef'=4] {'frame','dom'}, use_global_device_ids=true, to_apply=%region_2.3 | all-reduce | flops 15360 | bytes 122880 | tf_op jit(solution)/shard_map/psum | solution.py:85
  551.4 53.3 %while.54 = (s32[]{:T(128)}, f32[4096]{0:T(1024)S(1)}, s32[8,4096]{1,0:T(8,128)}, f32[8,4096]{1,0:T(8,128)}, f32[8,4096]{1,0:T(8,128)}, /*index=5*/s32[8,32]{1,0...) while((s32[]{:T(128)}, f32[4096]{0:T(1024)S(1)}, ...), condition=%wide.region_6.0_spmd, body=%wide.region_5.7_spmd.sunk | while | flops 30371208 | bytes 11859845 | solution.py:59
  553.2 4.2 select_add_fusion.8
  558.3 6.1 fusion.108
  566.5 4.2 select_add_fusion.8
  571.6 6.1 fusion.108
  578.1 0.8 fusion.106
  579.8 4.2 select_add_fusion.8
  585.0 6.1 fusion.108
  593.1 4.2 select_add_fusion.8
  598.3 6.1 fusion.108
  605.3 14.6 all-reduce
  620.5 256.4 %psum.59 = f32[]{:T(128)} all-reduce(f32[]{:T(128)} %multiply_reduce_fusion.3), channel_id=1, replica_groups=mesh['frame'=16,'dom'=8,'coef'=4] {'frame','dom'}, use_global_device_ids=true, to_apply=%region_9.11 | all-reduce | flops 1 | bytes 8 | tf_op jit(solution)/shard_map/psum | solution.py:99
  878.3 49.7 %while.57 = (s32[]{:T(128)}, f32[96,160]{0,1:T(8,128)S(1)}, s32[8,32]{1,0:T(8,128)}, f32[4096]{0:T(1024)S(1)}, s32[8,4096]{1,0:T(8,128)}, /*index=5*/f32[8,4096]...) while((s32[]{:T(128)}, f32[96,160]{0,1:T(8,128)S(1)}, ...), condition=%wide.region_11.13_spmd.clone, body=%wide.region_10.12_spmd.clone.sunk | while | flops 42192900 | bytes 11854863 | solution.py:75
  880.1 1.9 select_add_fusion.11
  882.0 8.4 fusion.124
  892.5 1.9 select_add_fusion.11
  894.4 8.4 fusion.124
  904.9 1.9 select_add_fusion.11
  906.9 8.4 fusion.124
  917.3 1.9 select_add_fusion.11
  919.3 8.4 fusion.124
  928.3 485.9 %psum.60 = f32[15360]{0:T(1024)S(1)} all-reduce(f32[15360]{0:T(1024)S(1)} %reshape.228), channel_id=1, replica_groups=mesh['frame'=16,'dom'=8,'coef'=4] {'frame','dom'}, use_global_device_ids=true, to_apply=%region_12.14 | all-reduce | flops 15360 | bytes 122880 | tf_op jit(solution)/shard_map/psum | solution.py:85
  1414.8 6.9 psum.61
  1423.1 53.3 %while.55 = (s32[]{:T(128)}, f32[4096]{0:T(1024)S(1)}, s32[8,4096]{1,0:T(8,128)}, f32[8,4096]{1,0:T(8,128)}, f32[8,4096]{1,0:T(8,128)}, /*index=5*/s32[8,32]{1,0...) while((s32[]{:T(128)}, f32[4096]{0:T(1024)S(1)}, ...), condition=%wide.region_16.18_spmd, body=%wide.region_15.17_spmd.sunk | while | flops 30371208 | bytes 11859845 | solution.py:59
  1424.8 4.2 select_add_fusion.9
  1430.0 6.1 fusion.113
  1436.4 0.8 fusion.111
  1438.2 4.2 select_add_fusion.9
  1443.3 6.1 fusion.113
  1451.5 4.2 select_add_fusion.9
  1456.6 6.1 fusion.113
  1464.8 4.2 select_add_fusion.9
  1470.0 6.1 fusion.113
  1476.4 12.1 psum.62
  1489.1 258.2 %psum.63 = f32[]{:T(128)} all-reduce(f32[]{:T(128)} %multiply_reduce_fusion.2), channel_id=1, replica_groups=mesh['frame'=16,'dom'=8,'coef'=4] {'frame','dom'}, use_global_device_ids=true, to_apply=%region_19.21 | all-reduce | flops 1 | bytes 8 | tf_op jit(solution)/shard_map/psum | solution.py:99
  (281 shorter events, 42.3 us)
Async XLA Ops:
  4.3 9.1 copy-start
  17.4 9.1 copy-start
  30.5 9.1 copy-start
  43.6 9.1 copy-start
  551.4 326.9 %copy-start.4 = (f32[4096]{0:T(1024)S(1)}, f32[4096]{0:T(1024)}, u32[]{:S(2)}) copy-start(f32[4096]{0:T(1024)} %get-tuple-element.1094) | copy-start | bytes 49156
  551.4 6.0 copy-start.1
  564.8 6.0 copy-start.1
  578.1 6.0 copy-start.1
  591.4 6.0 copy-start.1
  882.0 8.4 copy-start.2
  894.4 8.4 copy-start.2
  906.8 8.4 copy-start.2
  919.3 8.4 copy-start.2
  1423.1 6.0 copy-start.3
  1436.4 6.0 copy-start.3
  1449.8 6.0 copy-start.3
  1463.1 6.0 copy-start.3
where the time goes:
time: 1750 us
  blocking collectives  1530 us (87%)
  matrix products  118 us (7%)
  other arithmetic  78.9 us (5%)
    psum x2, blocking collectives, transpose_sum(): share = lax.psum(local, ('frame', 'dom'))  984 us
    psum x2, blocking collectives, on_device(): image_total = lax.psum(jnp.sum(image * image), ('frame', 'dom'))  515 us
    dot_general x8, matrix products, backward_step(): jnp.einsum('sktr,tr->stk', tiles, piece, precision=lax.Precision.HIGHEST)  66.9 us
    add x16, other arithmetic, dense_tiles(): tiles = tiles + jnp.where(hit, (geom * weight)[:, None, :], 0.0)  49.2 us
    dot_general x8, matrix products, forward_step(): jnp.einsum('sktr,stk->tr', tiles, chosen, precision=lax.Precision.HIGHEST)  49 us

commit v1 on v0

--- a/solution.py
+++ b/solution.py
@@ -82,7 +82,8 @@
         local = backward(resid, per_coef, geometry, fraction, interval, pattern).reshape(
             per_coef * NK
         )
-        share = lax.psum(local, ("frame", "dom"))
+        inner = lax.psum(local, "dom")
+        share = lax.psum(inner, "frame")
         total = lax.psum(jnp.sum(share * share), "coef")
         return (share, total)
 

time: 1750 us -> 925 us (0.53)
  blocking collectives: 1530 us -> 704 us
    psum x2 -> x4, blocking collectives: 984 us -> 133 us  [the longest x2 83.5 us: transpose_sum(): share = lax.psum(inner, 'frame')]
    psum x2, blocking collectives: 515 us -> 538 us  [on_device(): image_total = lax.psum(jnp.sum(image * image), ('frame', 'dom'))]
where the time goes in v1:
time: 925 us; the launch traced here: 922 us
  blocking collectives  704 us (76%)
  matrix products  118 us (13%)
  other arithmetic  78.9 us (9%)
  local copies, waits for them, and re-layouts  14.3 us (2%)
    psum x2, blocking collectives, on_device(): image_total = lax.psum(jnp.sum(image * image), ('frame', 'dom'))  538 us
    psum x2, blocking collectives, transpose_sum(): share = lax.psum(inner, 'frame')  83.5 us
    dot_general x8, matrix products, backward_step(): jnp.einsum('sktr,tr->stk', tiles, piece, precision=lax.Precision.HIGHEST)  66.9 us
    add x16, other arithmetic, dense_tiles(): tiles = tiles + jnp.where(hit, (geom * weight)[:, None, :], 0.0)  49.2 us
    psum x2, blocking collectives, transpose_sum(): inner = lax.psum(local, 'dom')  49.1 us
    dot_general x8, matrix products, forward_step(): jnp.einsum('sktr,stk->tr', tiles, chosen, precision=lax.Precision.HIGHEST)  49 us
    psum x2, blocking collectives, on_device(): image = lax.psum(partial_image, 'coef')  26.7 us

profile of v1, /device:TPU:1, one launch (start us, length us, event | category | flops | bytes accessed | tf_op | source)
XLA Modules:
  0.0 922.1 jit_solution(2606078066554333685)
XLA Ops:
  0.6 52.4 %while.56 = (s32[]{:T(128)}, f32[96,160]{0,1:T(8,128)S(1)}, s32[8,32]{1,0:T(8,128)}, f32[4096]{0:T(1024)}, s32[8,4096]{1,0:T(8,128)}, /*index=5*/f32[8,4096]{1,0...) while((s32[]{:T(128)}, f32[96,160]{0,1:T(8,128)S(1)}, ...), condition=%wide.region_1.2_spmd.clone, body=%wide.region_0.1_spmd.clone.sunk | while | flops 42192900 | bytes 11854863 | solution.py:75
  0.7 0.8 fusion.117
  2.4 1.9 select_add_fusion.10
  5.0 8.4 fusion.118
  15.5 1.9 select_add_fusion.10
  18.1 8.4 fusion.118
  26.9 0.8 fusion.117
  28.6 1.9 select_add_fusion.10
  31.2 8.4 fusion.118
  41.7 1.9 select_add_fusion.10
  44.3 8.4 fusion.118
  53.3 27.7 %psum.70 = f32[15360]{0:T(1024)S(1)} all-reduce(f32[15360]{0:T(1024)S(1)} %reshape.226), channel_id=1, replica_groups=mesh['frame'=16,'dom'=8,'coef'=4] {'dom'}, use_global_device_ids=true, to_apply=%region_2.3 | all-reduce | flops 15360 | bytes 122880 | tf_op jit(solution)/shard_map/psum | solution.py:85
  80.9 44.6 %psum.71 = f32[15360]{0:T(1024)S(1)} all-reduce(f32[15360]{0:T(1024)S(1)} %psum.70), channel_id=1, replica_groups=mesh['frame'=16,'dom'=8,'coef'=4] {'frame'}, use_global_device_ids=true, to_apply=%region_3.4 | all-reduce | flops 15360 | bytes 122880 | tf_op jit(solution)/shard_map/psum | solution.py:86
  125.6 53.3 %while.54 = (s32[]{:T(128)}, f32[4096]{0:T(1024)S(1)}, s32[8,4096]{1,0:T(8,128)}, f32[8,4096]{1,0:T(8,128)}, f32[8,4096]{1,0:T(8,128)}, /*index=5*/s32[8,32]{1,0...) while((s32[]{:T(128)}, f32[4096]{0:T(1024)S(1)}, ...), condition=%wide.region_7.0_spmd, body=%wide.region_6.8_spmd.sunk | while | flops 30371208 | bytes 11859845 | solution.py:59
  127.4 4.2 select_add_fusion.8
  132.5 6.1 fusion.108
  140.7 4.2 select_add_fusion.8
  145.8 6.1 fusion.108
  152.3 0.8 fusion.106
  154.0 4.2 select_add_fusion.8
  159.2 6.1 fusion.108
  167.3 4.2 select_add_fusion.8
  172.5 6.1 fusion.108
  179.5 14.6 %all-reduce = (f32[4096]{0:T(1024)S(1)}, f32[]{:T(128)}) all-reduce(f32[4096]{0:T(1024)S(1)} %get-tuple-element.530, f32[]{:T(128)} %multiply_reduce_fusion.1), channel_id=1, replica_groups=mesh['frame'=16,'dom'=8,'coef'=4] {'coef'}, use_global_device_ids=true, to_apply=%region_8.10 | all-reduce | flops 4097 | bytes 32776 | tf_op jit(solution)/shard_map/psum | solution.py:99
  194.7 268.3 %psum.74 = f32[]{:T(128)} all-reduce(f32[]{:T(128)} %multiply_reduce_fusion.3), channel_id=1, replica_groups=mesh['frame'=16,'dom'=8,'coef'=4] {'frame','dom'}, use_global_device_ids=true, to_apply=%region_10.12 | all-reduce | flops 1 | bytes 8 | tf_op jit(solution)/shard_map/psum | solution.py:100
  464.4 49.7 %while.57 = (s32[]{:T(128)}, f32[96,160]{0,1:T(8,128)S(1)}, s32[8,32]{1,0:T(8,128)}, f32[4096]{0:T(1024)S(1)}, s32[8,4096]{1,0:T(8,128)}, /*index=5*/f32[8,4096]...) while((s32[]{:T(128)}, f32[96,160]{0,1:T(8,128)S(1)}, ...), condition=%wide.region_12.14_spmd.clone, body=%wide.region_11.13_spmd.clone.sunk | while | flops 42192900 | bytes 11854863 | solution.py:75
  466.1 1.9 select_add_fusion.11
  468.1 8.4 fusion.124
  478.6 1.9 select_add_fusion.11
  480.5 8.4 fusion.124
  491.0 1.9 select_add_fusion.11
  492.9 8.4 fusion.124
  503.4 1.9 select_add_fusion.11
  505.4 8.4 fusion.124
  514.3 21.5 %psum.75 = f32[15360]{0:T(1024)S(1)} all-reduce(f32[15360]{0:T(1024)S(1)} %reshape.228), channel_id=1, replica_groups=mesh['frame'=16,'dom'=8,'coef'=4] {'dom'}, use_global_device_ids=true, to_apply=%region_13.15 | all-reduce | flops 15360 | bytes 122880 | tf_op jit(solution)/shard_map/psum | solution.py:85
  535.8 39.0 %psum.76 = f32[15360]{0:T(1024)S(1)} all-reduce(f32[15360]{0:T(1024)S(1)} %psum.75), channel_id=1, replica_groups=mesh['frame'=16,'dom'=8,'coef'=4] {'frame'}, use_global_device_ids=true, to_apply=%region_14.16 | all-reduce | flops 15360 | bytes 122880 | tf_op jit(solution)/shard_map/psum | solution.py:86
  575.4 7.2 psum.77
  584.0 53.3 %while.55 = (s32[]{:T(128)}, f32[4096]{0:T(1024)S(1)}, s32[8,4096]{1,0:T(8,128)}, f32[8,4096]{1,0:T(8,128)}, f32[8,4096]{1,0:T(8,128)}, /*index=5*/s32[8,32]{1,0...) while((s32[]{:T(128)}, f32[4096]{0:T(1024)S(1)}, ...), condition=%wide.region_18.20_spmd, body=%wide.region_17.19_spmd.sunk | while | flops 30371208 | bytes 11859845 | solution.py:59
  585.8 4.2 select_add_fusion.9
  590.9 6.1 fusion.113
  599.1 4.2 select_add_fusion.9
  604.2 6.1 fusion.113
  612.4 4.2 select_add_fusion.9
  617.6 6.1 fusion.113
  625.7 4.2 select_add_fusion.9
  630.9 6.1 fusion.113
  637.3 12.1 %psum.78 = f32[4096]{0:T(1024)S(1)} all-reduce(f32[4096]{0:T(1024)S(1)} %get-tuple-element.532), channel_id=1, replica_groups=mesh['frame'=16,'dom'=8,'coef'=4] {'coef'}, use_global_device_ids=true, to_apply=%region_19.21 | all-reduce | flops 4096 | bytes 32768 | tf_op jit(solution)/shard_map/psum | solution.py:99
  650.0 269.3 %psum.79 = f32[]{:T(128)} all-reduce(f32[]{:T(128)} %multiply_reduce_fusion.2), channel_id=1, replica_groups=mesh['frame'=16,'dom'=8,'coef'=4] {'frame','dom'}, use_global_device_ids=true, to_apply=%region_21.23 | all-reduce | flops 1 | bytes 8 | tf_op jit(solution)/shard_map/psum | solution.py:100
  (283 shorter events, 44.0 us)
Async XLA Ops:
  4.3 9.1 copy-start
  17.4 9.1 copy-start
  30.5 9.1 copy-start
  43.6 9.1 copy-start
  125.6 338.8 %copy-start.4 = (f32[4096]{0:T(1024)S(1)}, f32[4096]{0:T(1024)}, u32[]{:S(2)}) copy-start(f32[4096]{0:T(1024)} %get-tuple-element.1094) | copy-start | bytes 49156
  125.6 6.0 copy-start.1
  139.0 6.0 copy-start.1
  152.3 6.0 copy-start.1
  165.6 6.0 copy-start.1
  468.1 8.4 copy-start.2
  480.5 8.4 copy-start.2
  492.9 8.4 copy-start.2
  505.3 8.4 copy-start.2
  584.0 6.0 copy-start.3
  597.4 6.0 copy-start.3
  610.7 6.0 copy-start.3
  624.0 6.0 copy-start.3
